TPU v7x, 512 devices: a whole 4x4x16 slice. The times are simulated.
512 devices in a mesh: group: 8 (over y, x_lo), member: 64 (over z, x_hi, core).
Axes of the slice: x: 4 (x_hi: 2, x_lo: 2; x = x_hi * 2 + x_lo), y: 4, z: 16, core: 2. Of those that a mesh axis runs over, the one named last changes fastest.
Arguments:
- student: bfloat16 [196608, 768], P(('group', 'member')), may hold values from -0.29882812 to 0.29882812
- teacher: bfloat16 [196608, 1024], P(('group', 'member')), may hold values from -14 to 14
- counts: int32 [196608], P(('group', 'member')), may hold values from 1 to 7, as said below
- plan: int32 [8, 64, 5], P('group', 'member'), may hold values from 0 to 1, as said below
Outputs:
- grad_student: float32 [196608, 768], P(('group', 'member'))
- loss: float32 [], replicated
Inputs may be any that keep to these rules, and one draw needn't show every extreme that they name: `counts`: each row's count is a whole number from 1 up. The pairing is symmetric: plan[g, m, 2 + k - 1] equals plan[g, (m + k) mod 64, k - 1] for k = 1 to 2, and plan[g, m, 4] equals plan[g xor 1, m, 4].
All inputs are finite; a program needn't handle non-finite values.
Results may differ from a plain program's by a relative error of at most 0.0046.
Values may be sent and summed in bfloat16 or wider, within the bound.
A program may use at most 64 MiB of HBM per device.

v0:
```python
import jax
import jax.numpy as jnp
from jax import lax
from jax.sharding import PartitionSpec as P

EPS = 1e-06


def passed_along(value, axis, steps):
    count = lax.axis_size(axis)
    pairs = [(source, (source + steps) % count) for source in range(count)]
    return lax.ppermute(value, axis, pairs)


def partner_2(block, axis, bit):
    count = lax.axis_size(axis)
    route = []
    for low in range(count):
        high = low | 1 << bit
        if high != low and high < count:
            route += [(low, high), (high, low)]
    return lax.ppermute(block, axis, route)


def normalize(embeddings):
    widened = embeddings.astype(jnp.float32)
    row_scale = lax.rsqrt(jnp.sum(widened * widened, axis=-1, keepdims=True) + EPS)
    return ((widened * row_scale).astype(jnp.bfloat16), row_scale)


def block_terms(local_rows, partner, switch):
    local_s, local_t, local_w = local_rows
    partner_s, partner_t, partner_w = partner
    local_count = local_s.shape[0]
    features = local_s.shape[1]

    def compute(operand):
        student_sim = jnp.einsum(
            "id,jd->ij", local_s, partner_s, preferred_element_type=jnp.float32
        )
        teacher_sim = jnp.einsum(
            "id,jd->ij", local_t, partner_t, preferred_element_type=jnp.float32
        )
        mismatch = student_sim - teacher_sim
        pair_weight = local_w[:, None] * partner_w.astype(jnp.float32)[None, :]
        coefficient = (pair_weight * mismatch).astype(jnp.bfloat16)
        contrib = jnp.dot(coefficient, partner_s, preferred_element_type=jnp.float32)
        results = (contrib, jnp.sum(pair_weight * mismatch * mismatch), jnp.sum(pair_weight))
        return results

    def skipped(operand):
        results = (
            jnp.zeros((local_count, features), jnp.float32),
            jnp.float32(0.0),
            jnp.float32(0.0),
        )
        return results

    return lax.cond(switch > 0, compute, skipped, 0)


def per_device(student, teacher, counts, plan):
    unit_student, row_scale = normalize(student)
    unit_teacher, unused_scale = normalize(teacher)
    weights = counts.astype(jnp.float32)
    switches = plan.reshape(-1).astype(jnp.float32)
    span_blocks = (switches.shape[0] - 1) // 2
    local_rows = (unit_student, unit_teacher, weights)
    outgoing = (unit_student, unit_teacher, weights.astype(jnp.bfloat16))
    summed_grad, loss_sum, weight_sum = block_terms(local_rows, outgoing, jnp.float32(1.0))
    for offset in range(1, span_blocks + 1):
        lower = passed_along((outgoing[0], outgoing[1], outgoing[2]), "member", offset)
        upper = passed_along((outgoing[0], outgoing[1], outgoing[2]), "member", -offset)
        for column, partner in ((offset - 1, lower), (span_blocks + offset - 1, upper)):
            contrib, loss_part, weight_part = block_terms(local_rows, partner, switches[column])
            summed_grad = summed_grad + contrib
            loss_sum = loss_sum + loss_part
            weight_sum = weight_sum + weight_part
    partner = partner_2((outgoing[0], outgoing[1], outgoing[2]), "group", 0)
    contrib, loss_part, weight_part = block_terms(local_rows, partner, switches[2 * span_blocks])
    summed_grad = summed_grad + contrib
    loss_sum = loss_sum + loss_part
    weight_sum = weight_sum + weight_part
    loss_sum, weight_sum = lax.psum((loss_sum, weight_sum), ("group", "member"))
    unit_float = unit_student.astype(jnp.float32)
    along_unit = jnp.sum(summed_grad * unit_float, axis=-1, keepdims=True)
    grad_student = 4.0 * row_scale * (summed_grad - along_unit * unit_float)
    loss = student.shape[1] * loss_sum / weight_sum
    return (grad_student, loss)


def solution(mesh):
    return jax.shard_map(
        per_device,
        mesh=mesh,
        in_specs=(
            P(("group", "member"), None),
            P(("group", "member"), None),
            P(("group", "member")),
            P("group", "member", None),
        ),
        out_specs=(P(("group", "member"), None), P()),
        check_vma=False,
    )
```

profile of v0, /device:TPU:1, one launch (start us, length us, event | category | flops | bytes accessed | tf_op | source)
XLA Modules:
  0.0 263.8 jit_solution(1487551678774136010)
XLA Ops:
  2.4 6.0 %collective-permute-start.2 = (bf16[384,1024]{1,0:T(8,128)(2,1)S(1)}, bf16[384,1024]{1,0:T(8,128)(2,1)S(1)}, u32[]{:S(2)}, u32[]{:S(2)}) collective-permute-start(bf16[384,1024]{1,0:T(8,128)(2,1)S(1)} %fusion.36), channel_id=1, source_target_pairs={{0,1},{1,2},{2,3},{3,4},{4,5},{5,6},{6,7},{7,8},{8,9},{9,10},{10,1... | collective-permute-start | bytes 2359304 | tf_op jit(solution)/shard_map/ppermute | solution.py:12
  8.4 4.7 %collective-permute-start.5 = (bf16[384,1024]{1,0:T(8,128)(2,1)S(1)}, bf16[384,1024]{1,0:T(8,128)(2,1)S(1)}, u32[]{:S(2)}, u32[]{:S(2)}) collective-permute-start(bf16[384,1024]{1,0:T(8,128)(2,1)S(1)} %fusion.36), channel_id=1, source_target_pairs={{0,63},{1,0},{2,1},{3,2},{4,3},{5,4},{6,5},{7,6},{8,7},{9,8},{10,9... | collective-permute-start | bytes 2359304 | tf_op jit(solution)/shard_map/ppermute | solution.py:12
  13.1 2.4 collective-permute-start
  15.5 7.4 %collective-permute-start.3 = (bf16[384]{0:T(512)(128)(2,1)S(1)}, bf16[384]{0:T(512)(128)(2,1)S(1)}, u32[]{:S(2)}, u32[]{:S(2)}) collective-permute-start(bf16[384]{0:T(512)(128)(2,1)S(1)} %get-tuple-element.139), channel_id=1, source_target_pairs={{0,63},{1,0},{2,1},{3,2},{4,3},{5,4},{6,5},{7,6},{8,7},{9,8},{10,9... | collective-permute-start | bytes 2312 | tf_op jit(solution)/shard_map/ppermute | solution.py:12
  23.0 1.9 collective-permute-start.6
  25.8 5.9 %collective-permute-start.1 = (bf16[384,768]{1,0:T(8,128)(2,1)S(1)}, bf16[384,768]{1,0:T(8,128)(2,1)S(1)}, u32[]{:S(2)}, u32[]{:S(2)}) collective-permute-start(bf16[384,768]{1,0:T(8,128)(2,1)S(1)} %fusion.38), channel_id=1, source_target_pairs={{0,1},{1,2},{2,3},{3,4},{4,5},{5,6},{6,7},{7,8},{8,9},{9,10},{10,1... | collective-permute-start | bytes 1769480 | tf_op jit(solution)/shard_map/ppermute | solution.py:12
  31.7 7.7 %collective-permute-start.9 = (bf16[384]{0:T(512)(128)(2,1)S(1)}, bf16[384]{0:T(512)(128)(2,1)S(1)}, u32[]{:S(2)}, u32[]{:S(2)}) collective-permute-start(bf16[384]{0:T(512)(128)(2,1)S(1)} %get-tuple-element.139), channel_id=1, source_target_pairs={{0,62},{1,63},{2,0},{3,1},{4,2},{5,3},{6,4},{7,5},{8,6},{9,7},{10,... | collective-permute-start | bytes 2312 | tf_op jit(solution)/shard_map/ppermute | solution.py:12
  39.5 5.4 %collective-permute-start.4 = (bf16[384,768]{1,0:T(8,128)(2,1)S(1)}, bf16[384,768]{1,0:T(8,128)(2,1)S(1)}, u32[]{:S(2)}, u32[]{:S(2)}) collective-permute-start(bf16[384,768]{1,0:T(8,128)(2,1)S(1)} %fusion.38), channel_id=1, source_target_pairs={{0,63},{1,0},{2,1},{3,2},{4,3},{5,4},{6,5},{7,6},{8,7},{9,8},{10,9... | collective-permute-start | bytes 1769480 | tf_op jit(solution)/shard_map/ppermute | solution.py:12
  44.9 1.9 collective-permute-start.7
  46.9 1.9 collective-permute-start.8
  48.8 3.4 %collective-permute-done.4 = bf16[384,768]{1,0:T(8,128)(2,1)S(1)} collective-permute-done((bf16[384,768]{1,0:T(8,128)(2,1)S(1)}, bf16[384,768]{1,0:T(8,128)(2,1)S(1)}, u32[]{:S(2)}, u32[]{:S(2)}) %collective-permute-start.4) | collective-permute-done | bytes 589856 | tf_op jit(solution)/shard_map/ppermute | solution.py:12
  52.2 10.2 %collective-permute-start.11 = (bf16[384,1024]{1,0:T(8,128)(2,1)S(1)}, bf16[384,1024]{1,0:T(8,128)(2,1)}, u32[]{:S(2)}, u32[]{:S(2)}) collective-permute-start(bf16[384,1024]{1,0:T(8,128)(2,1)S(1)} %fusion.36), channel_id=1, source_target_pairs={{0,62},{1,63},{2,0},{3,1},{4,2},{5,3},{6,4},{7,5},{8,6},{9,7},{10,... | collective-permute-start | bytes 2359304 | tf_op jit(solution)/shard_map/ppermute | solution.py:12
  62.4 2.7 %collective-permute-done.7 = bf16[384,768]{1,0:T(8,128)(2,1)S(1)} collective-permute-done((bf16[384,768]{1,0:T(8,128)(2,1)S(1)}, bf16[384,768]{1,0:T(8,128)(2,1)S(1)}, u32[]{:S(2)}, u32[]{:S(2)}) %collective-permute-start.7) | collective-permute-done | bytes 589856 | tf_op jit(solution)/shard_map/ppermute | solution.py:12
  65.9 2.2 collective-permute-start.14
  68.1 27.2 %collective-permute-start.10 = (bf16[384,768]{1,0:T(8,128)(2,1)S(1)}, bf16[384,768]{1,0:T(8,128)(2,1)}, u32[]{:S(2)}, u32[]{:S(2)}) collective-permute-start(bf16[384,768]{1,0:T(8,128)(2,1)S(1)} %fusion.38), channel_id=1, source_target_pairs={{0,62},{1,63},{2,0},{3,1},{4,2},{5,3},{6,4},{7,5},{8,6},{9,7},{10,... | collective-permute-start | bytes 1769480 | tf_op jit(solution)/shard_map/ppermute | solution.py:12
  95.3 1.9 collective-permute-start.13
  101.7 2.0 multiply_reduce_fusion.5
  103.7 5.4 %conditional.5 = (f32[384,768]{1,0:T(8,128)S(1)}, f32[]{:T(128)}, f32[]{:T(128)}) conditional(s32[]{:T(128)} %bitcast, () %tuple.48, (f32[384]{0:T(512)S(1)}, bf16[384]{0:T(512)(128)(2,1)S(1)}, bf16[384,768]{1,0:T(8,128)(2,1)S(1)}, bf16[384,768]{1,0:T(8,128)(2,1)}, bf16[384,1024]{1,0:T(8,128)(2,1)S(1)}, ...), branch_computations={%region_2.0_spmd, %region_3.6_spmd} | conditional | flops 756302208 | bytes 12394840 | solution.py:59
  104.6 1.7 fusion.51
  109.8 3.4 %collective-permute-start.12 = (bf16[384]{0:T(512)(128)(2,1)S(1)}, bf16[384]{0:T(512)(128)(2,1)S(1)}, u32[]{:S(2)}, u32[]{:S(2)}) collective-permute-start(bf16[384]{0:T(512)(128)(2,1)S(1)} %get-tuple-element.139), channel_id=1, source_target_pairs={{0,64},{64,0},{128,192},{192,128},{256,320},{320,256},{384,448},{4... | collective-permute-start | bytes 2312 | tf_op jit(solution)/shard_map/ppermute | solution.py:22
  113.1 5.9 %conditional.6 = (f32[384,768]{1,0:T(8,128)}, f32[]{:T(128)}, f32[]{:T(128)}) conditional(s32[]{:T(128)} %bitcast.1, () %tuple.50, (f32[384]{0:T(512)S(1)}, bf16[384]{0:T(512)(128)(2,1)S(1)}, bf16[384,768]{1,0:T(8,128)(2,1)S(1)}, bf16[384,768]{1,0:T(8,128)(2,1)}, bf16[384,1024]{1,0:T(8,128)(2,1)S(1)}, /*index=5*/bf16[384,1024]{1,0:T(8,128)(2,1)}) %tuple.92), branch_computations={%region_6.7_spmd, %region_7.10_spmd} | conditional | flops 756302208 | bytes 9249084 | solution.py:59
  113.2 1.8 fusion.52
  119.0 4.7 %conditional.7 = (f32[384,768]{1,0:T(8,128)S(1)}, f32[]{:T(128)}, f32[]{:T(128)}) conditional(s32[]{:T(128)} %bitcast.2, () %tuple.52, (f32[384]{0:T(512)S(1)}, bf16[384]{0:T(512)(128)(2,1)S(1)}, bf16[384,768]{1,0:T(8,128)(2,1)S(1)}, bf16[384,768]{1,0:T(8,128)(2,1)}, bf16[384,1024]{1,0:T(8,128)(2,1)S(1)}, ...), branch_computations={%region_10.11_spmd, %region_11.14_spmd} | conditional | flops 756302208 | bytes 9249084 | solution.py:59
  119.1 1.8 fusion.53
  123.8 5.2 %collective-permute-done.10 = bf16[384,768]{1,0:T(8,128)(2,1)} collective-permute-done((bf16[384,768]{1,0:T(8,128)(2,1)S(1)}, bf16[384,768]{1,0:T(8,128)(2,1)}, u32[]{:S(2)}, u32[]{:S(2)}) %collective-permute-start.10) | collective-permute-done | bytes 589856 | tf_op jit(solution)/shard_map/ppermute | solution.py:12
  129.0 7.9 %conditional.8 = (f32[384,768]{1,0:T(8,128)}, f32[]{:T(128)}, f32[]{:T(128)}) conditional(s32[]{:T(128)} %bitcast.3, () %tuple.54, (f32[384]{0:T(512)S(1)}, bf16[384]{0:T(512)(128)(2,1)S(1)}, bf16[384,768]{1,0:T(8,128)(2,1)S(1)}, bf16[384,768]{1,0:T(8,128)(2,1)}, bf16[384,1024]{1,0:T(8,128)(2,1)S(1)}, /*index=5*/bf16[384,1024]{1,0:T(8,128)(2,1)}) %tuple.55), branch_computations={%region_14.15_spmd, %region_15.18_spmd} | conditional | flops 756302208 | bytes 6889760 | solution.py:59
  129.0 1.7 fusion.54
  130.7 2.3 multiply_reduce_fusion.3
  133.0 2.6 fusion.24
  138.1 1.6 fusion.45
  139.7 117.2 %all-reduce = (f32[]{:T(128)}, f32[]{:T(128)}) all-reduce(f32[]{:T(128)S(6)} %add.79, f32[]{:T(128)S(6)} %add.84), channel_id=1, replica_groups=mesh['group'=8,'member'=64] {'group','member'}, use_global_device_ids=true, to_apply=%region_24.0 | all-reduce | flops 2 | bytes 16 | tf_op jit(solution)/shard_map/psum | solution.py:84
  258.2 3.2 %fusion.39 = (f32[384]{0:T(512)S(1)}, f32[384,768]{1,0:T(8,128)S(1)}) fusion(f32[384,768]{1,0:T(8,128)} %copy-done.3, f32[384,768]{1,0:T(8,128)} %get-tuple-element.110, f32[384,768]{1,0:T(8,128)} %copy-done.2, f32[384,768]{1,0:T(8,128)} %get-tuple-element.108, f32[384,768]{1,0:T(8,128)S(1)} %fusion.45, f32[384,768]{1,0:T(8,128)} %copy-done.1, ...), kind=kLoop, calls=%fused_computation.56 | loop fusion | flops 3243648 | bytes 8850432 | tf_op jit(solution)/shard_map/reduce_sum | solution.py:86
  (65 shorter events, 13.4 us)
Async XLA Ops:
  0.6 1.5 copy-start.4
  0.6 12.4 %copy-start.13 = (s32[384]{0:T(512)S(1)}, s32[384]{0:T(512)}, u32[]{:S(2)}) copy-start(s32[384]{0:T(512)} %param.16) | copy-start | bytes 4612
  0.6 24.2 %copy-start = (bf16[384,768]{1,0:T(8,128)(2,1)S(1)}, bf16[384,768]{1,0:T(8,128)(2,1)}, u32[]{:S(2)}) copy-start(bf16[384,768]{1,0:T(8,128)(2,1)} %param.14) | copy-start | bytes 1769476
  2.3 65.8 %copy-start.14 = (s32[1,1,5]{2,1,0:T(1,128)S(1)}, s32[1,1,5]{2,1,0:T(1,128)}, u32[]{:S(2)}) copy-start(s32[1,1,5]{2,1,0:T(1,128)} %param.17) | copy-start | bytes 64
  2.4 65.8 %collective-permute-start.2 = (bf16[384,1024]{1,0:T(8,128)(2,1)S(1)}, bf16[384,1024]{1,0:T(8,128)(2,1)S(1)}, u32[]{:S(2)}, u32[]{:S(2)}) collective-permute-start(bf16[384,1024]{1,0:T(8,128)(2,1)S(1)} %fusion.36), channel_id=1, source_target_pairs={{0,1},{1,2},{2,3},{3,4},{4,5},{5,6},{6,7},{7,8},{8,9},{9,10},{10,1... | collective-permute-start | bytes 2359304 | tf_op jit(solution)/shard_map/ppermute | solution.py:12
  8.4 86.9 %collective-permute-start.5 = (bf16[384,1024]{1,0:T(8,128)(2,1)S(1)}, bf16[384,1024]{1,0:T(8,128)(2,1)S(1)}, u32[]{:S(2)}, u32[]{:S(2)}) collective-permute-start(bf16[384,1024]{1,0:T(8,128)(2,1)S(1)} %fusion.36), channel_id=1, source_target_pairs={{0,63},{1,0},{2,1},{3,2},{4,3},{5,4},{6,5},{7,6},{8,7},{9,8},{10,9... | collective-permute-start | bytes 2359304 | tf_op jit(solution)/shard_map/ppermute | solution.py:12
  13.1 12.7 %collective-permute-start = (bf16[384]{0:T(512)(128)(2,1)S(1)}, bf16[384]{0:T(512)(128)(2,1)S(1)}, u32[]{:S(2)}, u32[]{:S(2)}) collective-permute-start(bf16[384]{0:T(512)(128)(2,1)S(1)} %get-tuple-element.139), channel_id=1, source_target_pairs={{0,1},{1,2},{2,3},{3,4},{4,5},{5,6},{6,7},{7,8},{8,9},{9,10},{10,1... | collective-permute-start | bytes 2312 | tf_op jit(solution)/shard_map/ppermute | solution.py:12
  15.5 16.2 %collective-permute-start.3 = (bf16[384]{0:T(512)(128)(2,1)S(1)}, bf16[384]{0:T(512)(128)(2,1)S(1)}, u32[]{:S(2)}, u32[]{:S(2)}) collective-permute-start(bf16[384]{0:T(512)(128)(2,1)S(1)} %get-tuple-element.139), channel_id=1, source_target_pairs={{0,63},{1,0},{2,1},{3,2},{4,3},{5,4},{6,5},{7,6},{8,7},{9,8},{10,9... | collective-permute-start | bytes 2312 | tf_op jit(solution)/shard_map/ppermute | solution.py:12
  23.0 16.5 %collective-permute-start.6 = (bf16[384]{0:T(512)(128)(2,1)S(1)}, bf16[384]{0:T(512)(128)(2,1)S(1)}, u32[]{:S(2)}, u32[]{:S(2)}) collective-permute-start(bf16[384]{0:T(512)(128)(2,1)S(1)} %get-tuple-element.139), channel_id=1, source_target_pairs={{0,2},{1,3},{2,4},{3,5},{4,6},{5,7},{6,8},{7,9},{8,10},{9,11},{10,... | collective-permute-start | bytes 2312 | tf_op jit(solution)/shard_map/ppermute | solution.py:12
  25.8 21.1 %collective-permute-start.1 = (bf16[384,768]{1,0:T(8,128)(2,1)S(1)}, bf16[384,768]{1,0:T(8,128)(2,1)S(1)}, u32[]{:S(2)}, u32[]{:S(2)}) collective-permute-start(bf16[384,768]{1,0:T(8,128)(2,1)S(1)} %fusion.38), channel_id=1, source_target_pairs={{0,1},{1,2},{2,3},{3,4},{4,5},{5,6},{6,7},{7,8},{8,9},{9,10},{10,1... | collective-permute-start | bytes 1769480 | tf_op jit(solution)/shard_map/ppermute | solution.py:12
  31.7 13.2 %collective-permute-start.9 = (bf16[384]{0:T(512)(128)(2,1)S(1)}, bf16[384]{0:T(512)(128)(2,1)S(1)}, u32[]{:S(2)}, u32[]{:S(2)}) collective-permute-start(bf16[384]{0:T(512)(128)(2,1)S(1)} %get-tuple-element.139), channel_id=1, source_target_pairs={{0,62},{1,63},{2,0},{3,1},{4,2},{5,3},{6,4},{7,5},{8,6},{9,7},{10,... | collective-permute-start | bytes 2312 | tf_op jit(solution)/shard_map/ppermute | solution.py:12
  39.5 12.7 %collective-permute-start.4 = (bf16[384,768]{1,0:T(8,128)(2,1)S(1)}, bf16[384,768]{1,0:T(8,128)(2,1)S(1)}, u32[]{:S(2)}, u32[]{:S(2)}) collective-permute-start(bf16[384,768]{1,0:T(8,128)(2,1)S(1)} %fusion.38), channel_id=1, source_target_pairs={{0,63},{1,0},{2,1},{3,2},{4,3},{5,4},{6,5},{7,6},{8,7},{9,8},{10,9... | collective-permute-start | bytes 1769480 | tf_op jit(solution)/shard_map/ppermute | solution.py:12
  44.9 20.1 %collective-permute-start.7 = (bf16[384,768]{1,0:T(8,128)(2,1)S(1)}, bf16[384,768]{1,0:T(8,128)(2,1)S(1)}, u32[]{:S(2)}, u32[]{:S(2)}) collective-permute-start(bf16[384,768]{1,0:T(8,128)(2,1)S(1)} %fusion.38), channel_id=1, source_target_pairs={{0,2},{1,3},{2,4},{3,5},{4,6},{5,7},{6,8},{7,9},{8,10},{9,11},{10,... | collective-permute-start | bytes 1769480 | tf_op jit(solution)/shard_map/ppermute | solution.py:12
  46.8 18.2 %copy-start.9 = (bf16[384,768]{1,0:T(8,128)(2,1)}, bf16[384,768]{1,0:T(8,128)(2,1)S(1)}, u32[]{:S(2)}) copy-start(bf16[384,768]{1,0:T(8,128)(2,1)S(1)} %collective-permute-done.1) | copy-start | bytes 1769476
  46.9 62.9 %collective-permute-start.8 = (bf16[384,1024]{1,0:T(8,128)(2,1)S(1)}, bf16[384,1024]{1,0:T(8,128)(2,1)}, u32[]{:S(2)}, u32[]{:S(2)}) collective-permute-start(bf16[384,1024]{1,0:T(8,128)(2,1)S(1)} %fusion.36), channel_id=1, source_target_pairs={{0,2},{1,3},{2,4},{3,5},{4,6},{5,7},{6,8},{7,9},{8,10},{9,11},{10,... | collective-permute-start | bytes 2359304 | tf_op jit(solution)/shard_map/ppermute | solution.py:12
  52.2 12.9 %copy-start.7 = (bf16[384,768]{1,0:T(8,128)(2,1)}, bf16[384,768]{1,0:T(8,128)(2,1)S(1)}, u32[]{:S(2)}) copy-start(bf16[384,768]{1,0:T(8,128)(2,1)S(1)} %collective-permute-done.4) | copy-start | bytes 1769476
  52.2 76.8 %collective-permute-start.11 = (bf16[384,1024]{1,0:T(8,128)(2,1)S(1)}, bf16[384,1024]{1,0:T(8,128)(2,1)}, u32[]{:S(2)}, u32[]{:S(2)}) collective-permute-start(bf16[384,1024]{1,0:T(8,128)(2,1)S(1)} %fusion.36), channel_id=1, source_target_pairs={{0,62},{1,63},{2,0},{3,1},{4,2},{5,3},{6,4},{7,5},{8,6},{9,7},{10,... | collective-permute-start | bytes 2359304 | tf_op jit(solution)/shard_map/ppermute | solution.py:12
  65.0 0.8 copy-start.5
  65.9 71.1 %collective-permute-start.14 = (bf16[384,1024]{1,0:T(8,128)(2,1)S(1)}, bf16[384,1024]{1,0:T(8,128)(2,1)}, u32[]{:S(2)}, u32[]{:S(2)}) collective-permute-start(bf16[384,1024]{1,0:T(8,128)(2,1)S(1)} %fusion.36), channel_id=1, source_target_pairs={{0,64},{64,0},{128,192},{192,128},{256,320},{320,256},{384,448},{4... | collective-permute-start | bytes 2359304 | tf_op jit(solution)/shard_map/ppermute | solution.py:22
  68.1 60.8 %collective-permute-start.10 = (bf16[384,768]{1,0:T(8,128)(2,1)S(1)}, bf16[384,768]{1,0:T(8,128)(2,1)}, u32[]{:S(2)}, u32[]{:S(2)}) collective-permute-start(bf16[384,768]{1,0:T(8,128)(2,1)S(1)} %fusion.38), channel_id=1, source_target_pairs={{0,62},{1,63},{2,0},{3,1},{4,2},{5,3},{6,4},{7,5},{8,6},{9,7},{10,... | collective-permute-start | bytes 1769480 | tf_op jit(solution)/shard_map/ppermute | solution.py:12
  95.3 5.8 %copy-start.11 = (bf16[384,1024]{1,0:T(8,128)(2,1)}, bf16[384,1024]{1,0:T(8,128)(2,1)S(1)}, u32[]{:S(2)}) copy-start(bf16[384,1024]{1,0:T(8,128)(2,1)S(1)} %collective-permute-done.5) | copy-start | bytes 2359300
  95.3 41.6 %collective-permute-start.13 = (bf16[384,768]{1,0:T(8,128)(2,1)S(1)}, bf16[384,768]{1,0:T(8,128)(2,1)}, u32[]{:S(2)}, u32[]{:S(2)}) collective-permute-start(bf16[384,768]{1,0:T(8,128)(2,1)S(1)} %fusion.38), channel_id=1, source_target_pairs={{0,64},{64,0},{128,192},{192,128},{256,320},{320,256},{384,448},{4... | collective-permute-start | bytes 1769480 | tf_op jit(solution)/shard_map/ppermute | solution.py:22
  103.7 0.9 copy-start.12
  103.7 2.6 copy-start.10
  109.1 4.0 %copy-start.1 = (f32[384,768]{1,0:T(8,128)}, f32[384,768]{1,0:T(8,128)S(1)}, u32[]{:S(2)}) copy-start(f32[384,768]{1,0:T(8,128)S(1)} %get-tuple-element.107) | copy-start | bytes 3538948
  109.8 27.2 %collective-permute-start.12 = (bf16[384]{0:T(512)(128)(2,1)S(1)}, bf16[384]{0:T(512)(128)(2,1)S(1)}, u32[]{:S(2)}, u32[]{:S(2)}) collective-permute-start(bf16[384]{0:T(512)(128)(2,1)S(1)} %get-tuple-element.139), channel_id=1, source_target_pairs={{0,64},{64,0},{128,192},{192,128},{256,320},{320,256},{384,448},{4... | collective-permute-start | bytes 2312 | tf_op jit(solution)/shard_map/ppermute | solution.py:22
  113.2 1.8 copy-start.8
  119.0 1.8 copy-start.6
  123.8 5.2 %copy-start.2 = (f32[384,768]{1,0:T(8,128)}, f32[384,768]{1,0:T(8,128)S(1)}, u32[]{:S(2)}) copy-start(f32[384,768]{1,0:T(8,128)S(1)} %get-tuple-element.109) | copy-start | bytes 3538948
  137.1 1.0 copy-start.3
where the time goes:
time: 265 us; the launch traced here: 264 us
  blocking collectives  117 us (44%)
  starting transfers between devices  90.2 us (34%)
  matrix products  22 us (8%)
  waiting for transfers between devices  11.8 us (4%)
  between operations  7.98 us (3%)
  other arithmetic  6.54 us (2%)
  loops' own time  5.19 us (2%)
  local copies, waits for them, and re-layouts  2.83 us (1%)
    psum x1, blocking collectives, per_device(): loss_sum, weight_sum = lax.psum((loss_sum, weight_sum), ('group', 'member'))  117 us
    ppermute x12, starting transfers between devices, passed_along(): return lax.ppermute(value, axis, pairs)  82.7 us
    ppermute x12, waiting for transfers between devices, passed_along(): return lax.ppermute(value, axis, pairs)  11.8 us
    dot_general x5, matrix products, compute(): jnp.einsum('id,jd->ij', local_s, partner_s, preferred_element_type=jnp.fl...  7.7 us
    dot_general x5, matrix products, compute(): jnp.einsum('id,jd->ij', local_t, partner_t, preferred_element_type=jnp.fl...  7.59 us
    ppermute x3, starting transfers between devices, partner_2(): return lax.ppermute(block, axis, route)  7.5 us
    dot_general x5, matrix products, compute(): jnp.dot(coefficient, partner_s, preferred_element_type=jnp.float32)  6.75 us
  transfers between devices with their start and end apart: 15, of which 4 were waited for; matrix products, arithmetic and copies ran while one was open for 8% of the time, Pallas kernels for 0%

commit v1 on v0

--- a/solution.py
+++ b/solution.py
@@ -4,6 +4,11 @@
 from jax.sharding import PartitionSpec as P
 
 EPS = 1e-06
+
+
+def advance_patch_by_axis(w_in):
+    oldest = lax.psum(lax.psum(w_in, axis_name="group"), axis_name="member")
+    return oldest
 
 
 def passed_along(value, axis, steps):
@@ -81,7 +86,7 @@
     summed_grad = summed_grad + contrib
     loss_sum = loss_sum + loss_part
     weight_sum = weight_sum + weight_part
-    loss_sum, weight_sum = lax.psum((loss_sum, weight_sum), ("group", "member"))
+    loss_sum, weight_sum = advance_patch_by_axis((loss_sum, weight_sum))
     unit_float = unit_student.astype(jnp.float32)
     along_unit = jnp.sum(summed_grad * unit_float, axis=-1, keepdims=True)
     grad_student = 4.0 * row_scale * (summed_grad - along_unit * unit_float)

time: 265 us -> 305 us (1.15)
  blocking collectives: 117 us -> 156 us
    psum x1 -> x2, blocking collectives: 117 us -> 156 us  [advance_patch_by_axis(): oldest = lax.psum(lax.psum(w_in, axis_name='group'), axis_name='member')]
  transfers between devices with their start and end apart: 15 -> 15, of which waited for: 4 -> 4; matrix products, arithmetic and copies ran while one was open for 8% -> 7% of each run, Pallas kernels for 0% -> 0%
where the time goes in v1:
time: 305 us; the launch traced here: 303 us
  blocking collectives  156 us (51%)
  starting transfers between devices  90.2 us (30%)
  matrix products  22.1 us (7%)
  waiting for transfers between devices  11.8 us (4%)
  between operations  7.73 us (3%)
  other arithmetic  6.54 us (2%)
  loops' own time  5.3 us (2%)
    psum x2, blocking collectives, advance_patch_by_axis(): oldest = lax.psum(lax.psum(w_in, axis_name='group'), axis_name='member')  156 us
    ppermute x12, starting transfers between devices, passed_along(): return lax.ppermute(value, axis, pairs)  82.7 us
    ppermute x12, waiting for transfers between devices, passed_along(): return lax.ppermute(value, axis, pairs)  11.8 us
    dot_general x5, matrix products, compute(): jnp.einsum('id,jd->ij', local_s, partner_s, preferred_element_type=jnp.fl...  7.72 us
    dot_general x5, matrix products, compute(): jnp.einsum('id,jd->ij', local_t, partner_t, preferred_element_type=jnp.fl...  7.6 us
    ppermute x3, starting transfers between devices, partner_2(): return lax.ppermute(block, axis, route)  7.49 us
    dot_general x5, matrix products, compute(): jnp.dot(coefficient, partner_s, preferred_element_type=jnp.float32)  6.73 us
  transfers between devices with their start and end apart: 15, of which 4 were waited for; matrix products, arithmetic and copies ran while one was open for 7% of the time, Pallas kernels for 0%

profile of v1, /device:TPU:1, one launch (start us, length us, event | category | flops | bytes accessed | tf_op | source)
XLA Modules:
  0.0 303.0 jit_solution(12060177593051732516)
XLA Ops:
  2.4 6.0 %collective-permute-start.2 = (bf16[384,1024]{1,0:T(8,128)(2,1)S(1)}, bf16[384,1024]{1,0:T(8,128)(2,1)S(1)}, u32[]{:S(2)}, u32[]{:S(2)}) collective-permute-start(bf16[384,1024]{1,0:T(8,128)(2,1)S(1)} %fusion.36), channel_id=1, source_target_pairs={{0,1},{1,2},{2,3},{3,4},{4,5},{5,6},{6,7},{7,8},{8,9},{9,10},{10,1... | collective-permute-start | bytes 2359304 | tf_op jit(solution)/shard_map/ppermute | solution.py:17
  8.4 4.7 %collective-permute-start.5 = (bf16[384,1024]{1,0:T(8,128)(2,1)S(1)}, bf16[384,1024]{1,0:T(8,128)(2,1)S(1)}, u32[]{:S(2)}, u32[]{:S(2)}) collective-permute-start(bf16[384,1024]{1,0:T(8,128)(2,1)S(1)} %fusion.36), channel_id=1, source_target_pairs={{0,63},{1,0},{2,1},{3,2},{4,3},{5,4},{6,5},{7,6},{8,7},{9,8},{10,9... | collective-permute-start | bytes 2359304 | tf_op jit(solution)/shard_map/ppermute | solution.py:17
  13.1 2.4 collective-permute-start
  15.5 7.4 %collective-permute-start.3 = (bf16[384]{0:T(512)(128)(2,1)S(1)}, bf16[384]{0:T(512)(128)(2,1)S(1)}, u32[]{:S(2)}, u32[]{:S(2)}) collective-permute-start(bf16[384]{0:T(512)(128)(2,1)S(1)} %get-tuple-element.141), channel_id=1, source_target_pairs={{0,63},{1,0},{2,1},{3,2},{4,3},{5,4},{6,5},{7,6},{8,7},{9,8},{10,9... | collective-permute-start | bytes 2312 | tf_op jit(solution)/shard_map/ppermute | solution.py:17
  23.0 1.9 collective-permute-start.6
  25.8 5.9 %collective-permute-start.1 = (bf16[384,768]{1,0:T(8,128)(2,1)S(1)}, bf16[384,768]{1,0:T(8,128)(2,1)S(1)}, u32[]{:S(2)}, u32[]{:S(2)}) collective-permute-start(bf16[384,768]{1,0:T(8,128)(2,1)S(1)} %fusion.38), channel_id=1, source_target_pairs={{0,1},{1,2},{2,3},{3,4},{4,5},{5,6},{6,7},{7,8},{8,9},{9,10},{10,1... | collective-permute-start | bytes 1769480 | tf_op jit(solution)/shard_map/ppermute | solution.py:17
  31.7 7.7 %collective-permute-start.9 = (bf16[384]{0:T(512)(128)(2,1)S(1)}, bf16[384]{0:T(512)(128)(2,1)S(1)}, u32[]{:S(2)}, u32[]{:S(2)}) collective-permute-start(bf16[384]{0:T(512)(128)(2,1)S(1)} %get-tuple-element.141), channel_id=1, source_target_pairs={{0,62},{1,63},{2,0},{3,1},{4,2},{5,3},{6,4},{7,5},{8,6},{9,7},{10,... | collective-permute-start | bytes 2312 | tf_op jit(solution)/shard_map/ppermute | solution.py:17
  39.5 5.4 %collective-permute-start.4 = (bf16[384,768]{1,0:T(8,128)(2,1)S(1)}, bf16[384,768]{1,0:T(8,128)(2,1)S(1)}, u32[]{:S(2)}, u32[]{:S(2)}) collective-permute-start(bf16[384,768]{1,0:T(8,128)(2,1)S(1)} %fusion.38), channel_id=1, source_target_pairs={{0,63},{1,0},{2,1},{3,2},{4,3},{5,4},{6,5},{7,6},{8,7},{9,8},{10,9... | collective-permute-start | bytes 1769480 | tf_op jit(solution)/shard_map/ppermute | solution.py:17
  44.9 1.9 collective-permute-start.7
  46.9 1.9 collective-permute-start.8
  48.8 3.4 %collective-permute-done.4 = bf16[384,768]{1,0:T(8,128)(2,1)S(1)} collective-permute-done((bf16[384,768]{1,0:T(8,128)(2,1)S(1)}, bf16[384,768]{1,0:T(8,128)(2,1)S(1)}, u32[]{:S(2)}, u32[]{:S(2)}) %collective-permute-start.4) | collective-permute-done | bytes 589856 | tf_op jit(solution)/shard_map/ppermute | solution.py:17
  52.2 10.2 %collective-permute-start.11 = (bf16[384,1024]{1,0:T(8,128)(2,1)S(1)}, bf16[384,1024]{1,0:T(8,128)(2,1)}, u32[]{:S(2)}, u32[]{:S(2)}) collective-permute-start(bf16[384,1024]{1,0:T(8,128)(2,1)S(1)} %fusion.36), channel_id=1, source_target_pairs={{0,62},{1,63},{2,0},{3,1},{4,2},{5,3},{6,4},{7,5},{8,6},{9,7},{10,... | collective-permute-start | bytes 2359304 | tf_op jit(solution)/shard_map/ppermute | solution.py:17
  62.4 2.7 collective-permute-done.7
  65.9 2.2 collective-permute-start.14
  68.1 27.2 %collective-permute-start.10 = (bf16[384,768]{1,0:T(8,128)(2,1)S(1)}, bf16[384,768]{1,0:T(8,128)(2,1)}, u32[]{:S(2)}, u32[]{:S(2)}) collective-permute-start(bf16[384,768]{1,0:T(8,128)(2,1)S(1)} %fusion.38), channel_id=1, source_target_pairs={{0,62},{1,63},{2,0},{3,1},{4,2},{5,3},{6,4},{7,5},{8,6},{9,7},{10,... | collective-permute-start | bytes 1769480 | tf_op jit(solution)/shard_map/ppermute | solution.py:17
  95.3 1.9 collective-permute-start.13
  101.7 1.9 multiply_reduce_fusion.5
  103.6 5.5 %conditional.5 = (f32[384,768]{1,0:T(8,128)S(1)}, f32[]{:T(128)}, f32[]{:T(128)}) conditional(s32[]{:T(128)} %bitcast, () %tuple.48, (f32[384]{0:T(512)S(1)}, bf16[384]{0:T(512)(128)(2,1)S(1)}, bf16[384,768]{1,0:T(8,128)(2,1)S(1)}, bf16[384,768]{1,0:T(8,128)(2,1)}, bf16[384,1024]{1,0:T(8,128)(2,1)S(1)}, ...), branch_computations={%region_2.0_spmd, %region_3.6_spmd} | conditional | flops 756302208 | bytes 12394840 | solution.py:64
  104.5 1.7 fusion.51
  109.7 3.4 %collective-permute-start.12 = (bf16[384]{0:T(512)(128)(2,1)S(1)}, bf16[384]{0:T(512)(128)(2,1)S(1)}, u32[]{:S(2)}, u32[]{:S(2)}) collective-permute-start(bf16[384]{0:T(512)(128)(2,1)S(1)} %get-tuple-element.141), channel_id=1, source_target_pairs={{0,64},{64,0},{128,192},{192,128},{256,320},{320,256},{384,448},{4... | collective-permute-start | bytes 2312 | tf_op jit(solution)/shard_map/ppermute | solution.py:27
  113.1 5.9 %conditional.6 = (f32[384,768]{1,0:T(8,128)}, f32[]{:T(128)}, f32[]{:T(128)}) conditional(s32[]{:T(128)} %bitcast.1, () %tuple.50, (f32[384]{0:T(512)S(1)}, bf16[384]{0:T(512)(128)(2,1)S(1)}, bf16[384,768]{1,0:T(8,128)(2,1)S(1)}, bf16[384,768]{1,0:T(8,128)(2,1)}, bf16[384,1024]{1,0:T(8,128)(2,1)S(1)}, /*index=5*/bf16[384,1024]{1,0:T(8,128)(2,1)}) %tuple.92), branch_computations={%region_6.7_spmd, %region_7.10_spmd} | conditional | flops 756302208 | bytes 9249084 | solution.py:64
  113.1 1.8 fusion.52
  119.0 4.8 %conditional.7 = (f32[384,768]{1,0:T(8,128)S(1)}, f32[]{:T(128)}, f32[]{:T(128)}) conditional(s32[]{:T(128)} %bitcast.2, () %tuple.52, (f32[384]{0:T(512)S(1)}, bf16[384]{0:T(512)(128)(2,1)S(1)}, bf16[384,768]{1,0:T(8,128)(2,1)S(1)}, bf16[384,768]{1,0:T(8,128)(2,1)}, bf16[384,1024]{1,0:T(8,128)(2,1)S(1)}, ...), branch_computations={%region_10.11_spmd, %region_11.14_spmd} | conditional | flops 756302208 | bytes 9249084 | solution.py:64
  119.0 1.8 fusion.53
  123.8 5.2 %collective-permute-done.10 = bf16[384,768]{1,0:T(8,128)(2,1)} collective-permute-done((bf16[384,768]{1,0:T(8,128)(2,1)S(1)}, bf16[384,768]{1,0:T(8,128)(2,1)}, u32[]{:S(2)}, u32[]{:S(2)}) %collective-permute-start.10) | collective-permute-done | bytes 589856 | tf_op jit(solution)/shard_map/ppermute | solution.py:17
  129.0 7.9 %conditional.8 = (f32[384,768]{1,0:T(8,128)}, f32[]{:T(128)}, f32[]{:T(128)}) conditional(s32[]{:T(128)} %bitcast.3, () %tuple.54, (f32[384]{0:T(512)S(1)}, bf16[384]{0:T(512)(128)(2,1)S(1)}, bf16[384,768]{1,0:T(8,128)(2,1)S(1)}, bf16[384,768]{1,0:T(8,128)(2,1)}, bf16[384,1024]{1,0:T(8,128)(2,1)S(1)}, /*index=5*/bf16[384,1024]{1,0:T(8,128)(2,1)}) %tuple.55), branch_computations={%region_14.15_spmd, %region_15.18_spmd} | conditional | flops 756302208 | bytes 6889760 | solution.py:64
  129.0 1.7 fusion.54
  130.7 2.3 multiply_reduce_fusion.3
  133.0 2.6 fusion.24
  139.7 22.6 %all-reduce.1 = (f32[]{:T(128)}, f32[]{:T(128)}) all-reduce(f32[]{:T(128)S(6)} %add.83, f32[]{:T(128)S(6)} %add.88), channel_id=1, replica_groups=mesh['group'=8,'member'=64] {'group'}, use_global_device_ids=true, to_apply=%region_24.0 | all-reduce | flops 2 | bytes 16 | tf_op jit(solution)/shard_map/psum | solution.py:10
  162.2 133.9 %all-reduce = (f32[]{:T(128)}, f32[]{:T(128)}) all-reduce(f32[]{:T(128)} %get-tuple-element.136, f32[]{:T(128)} %get-tuple-element.137), channel_id=1, replica_groups=mesh['group'=8,'member'=64] {'member'}, use_global_device_ids=true, to_apply=%region_25.0 | all-reduce | flops 2 | bytes 16 | tf_op jit(solution)/shard_map/psum | solution.py:10
  297.4 3.2 %fusion.39 = (f32[384]{0:T(512)S(1)}, f32[384,768]{1,0:T(8,128)S(1)}) fusion(f32[384,768]{1,0:T(8,128)} %copy-done.3, f32[384,768]{1,0:T(8,128)} %get-tuple-element.110, f32[384,768]{1,0:T(8,128)} %copy-done.2, f32[384,768]{1,0:T(8,128)} %get-tuple-element.108, f32[384,768]{1,0:T(8,128)S(1)} %fusion.45, f32[384,768]{1,0:T(8,128)} %copy-done.1, ...), kind=kLoop, calls=%fused_computation.56 | loop fusion | flops 3243648 | bytes 8850432 | tf_op jit(solution)/shard_map/reduce_sum | solution.py:91
  (66 shorter events, 15.2 us)
Async XLA Ops:
  0.6 1.5 copy-start.4
  0.6 12.4 %copy-start.13 = (s32[384]{0:T(512)S(1)}, s32[384]{0:T(512)}, u32[]{:S(2)}) copy-start(s32[384]{0:T(512)} %param.16) | copy-start | bytes 4612
  0.6 24.2 %copy-start = (bf16[384,768]{1,0:T(8,128)(2,1)S(1)}, bf16[384,768]{1,0:T(8,128)(2,1)}, u32[]{:S(2)}) copy-start(bf16[384,768]{1,0:T(8,128)(2,1)} %param.14) | copy-start | bytes 1769476
  2.3 65.7 %copy-start.14 = (s32[1,1,5]{2,1,0:T(1,128)S(1)}, s32[1,1,5]{2,1,0:T(1,128)}, u32[]{:S(2)}) copy-start(s32[1,1,5]{2,1,0:T(1,128)} %param.17) | copy-start | bytes 64
  2.4 65.8 %collective-permute-start.2 = (bf16[384,1024]{1,0:T(8,128)(2,1)S(1)}, bf16[384,1024]{1,0:T(8,128)(2,1)S(1)}, u32[]{:S(2)}, u32[]{:S(2)}) collective-permute-start(bf16[384,1024]{1,0:T(8,128)(2,1)S(1)} %fusion.36), channel_id=1, source_target_pairs={{0,1},{1,2},{2,3},{3,4},{4,5},{5,6},{6,7},{7,8},{8,9},{9,10},{10,1... | collective-permute-start | bytes 2359304 | tf_op jit(solution)/shard_map/ppermute | solution.py:17
  8.4 86.9 %collective-permute-start.5 = (bf16[384,1024]{1,0:T(8,128)(2,1)S(1)}, bf16[384,1024]{1,0:T(8,128)(2,1)S(1)}, u32[]{:S(2)}, u32[]{:S(2)}) collective-permute-start(bf16[384,1024]{1,0:T(8,128)(2,1)S(1)} %fusion.36), channel_id=1, source_target_pairs={{0,63},{1,0},{2,1},{3,2},{4,3},{5,4},{6,5},{7,6},{8,7},{9,8},{10,9... | collective-permute-start | bytes 2359304 | tf_op jit(solution)/shard_map/ppermute | solution.py:17
  13.1 12.7 %collective-permute-start = (bf16[384]{0:T(512)(128)(2,1)S(1)}, bf16[384]{0:T(512)(128)(2,1)S(1)}, u32[]{:S(2)}, u32[]{:S(2)}) collective-permute-start(bf16[384]{0:T(512)(128)(2,1)S(1)} %get-tuple-element.141), channel_id=1, source_target_pairs={{0,1},{1,2},{2,3},{3,4},{4,5},{5,6},{6,7},{7,8},{8,9},{9,10},{10,1... | collective-permute-start | bytes 2312 | tf_op jit(solution)/shard_map/ppermute | solution.py:17
  15.5 16.2 %collective-permute-start.3 = (bf16[384]{0:T(512)(128)(2,1)S(1)}, bf16[384]{0:T(512)(128)(2,1)S(1)}, u32[]{:S(2)}, u32[]{:S(2)}) collective-permute-start(bf16[384]{0:T(512)(128)(2,1)S(1)} %get-tuple-element.141), channel_id=1, source_target_pairs={{0,63},{1,0},{2,1},{3,2},{4,3},{5,4},{6,5},{7,6},{8,7},{9,8},{10,9... | collective-permute-start | bytes 2312 | tf_op jit(solution)/shard_map/ppermute | solution.py:17
  23.0 16.5 %collective-permute-start.6 = (bf16[384]{0:T(512)(128)(2,1)S(1)}, bf16[384]{0:T(512)(128)(2,1)S(1)}, u32[]{:S(2)}, u32[]{:S(2)}) collective-permute-start(bf16[384]{0:T(512)(128)(2,1)S(1)} %get-tuple-element.141), channel_id=1, source_target_pairs={{0,2},{1,3},{2,4},{3,5},{4,6},{5,7},{6,8},{7,9},{8,10},{9,11},{10,... | collective-permute-start | bytes 2312 | tf_op jit(solution)/shard_map/ppermute | solution.py:17
  25.8 21.1 %collective-permute-start.1 = (bf16[384,768]{1,0:T(8,128)(2,1)S(1)}, bf16[384,768]{1,0:T(8,128)(2,1)S(1)}, u32[]{:S(2)}, u32[]{:S(2)}) collective-permute-start(bf16[384,768]{1,0:T(8,128)(2,1)S(1)} %fusion.38), channel_id=1, source_target_pairs={{0,1},{1,2},{2,3},{3,4},{4,5},{5,6},{6,7},{7,8},{8,9},{9,10},{10,1... | collective-permute-start | bytes 1769480 | tf_op jit(solution)/shard_map/ppermute | solution.py:17
  31.7 13.2 %collective-permute-start.9 = (bf16[384]{0:T(512)(128)(2,1)S(1)}, bf16[384]{0:T(512)(128)(2,1)S(1)}, u32[]{:S(2)}, u32[]{:S(2)}) collective-permute-start(bf16[384]{0:T(512)(128)(2,1)S(1)} %get-tuple-element.141), channel_id=1, source_target_pairs={{0,62},{1,63},{2,0},{3,1},{4,2},{5,3},{6,4},{7,5},{8,6},{9,7},{10,... | collective-permute-start | bytes 2312 | tf_op jit(solution)/shard_map/ppermute | solution.py:17
  39.5 12.7 %collective-permute-start.4 = (bf16[384,768]{1,0:T(8,128)(2,1)S(1)}, bf16[384,768]{1,0:T(8,128)(2,1)S(1)}, u32[]{:S(2)}, u32[]{:S(2)}) collective-permute-start(bf16[384,768]{1,0:T(8,128)(2,1)S(1)} %fusion.38), channel_id=1, source_target_pairs={{0,63},{1,0},{2,1},{3,2},{4,3},{5,4},{6,5},{7,6},{8,7},{9,8},{10,9... | collective-permute-start | bytes 1769480 | tf_op jit(solution)/shard_map/ppermute | solution.py:17
  44.9 20.1 %collective-permute-start.7 = (bf16[384,768]{1,0:T(8,128)(2,1)S(1)}, bf16[384,768]{1,0:T(8,128)(2,1)S(1)}, u32[]{:S(2)}, u32[]{:S(2)}) collective-permute-start(bf16[384,768]{1,0:T(8,128)(2,1)S(1)} %fusion.38), channel_id=1, source_target_pairs={{0,2},{1,3},{2,4},{3,5},{4,6},{5,7},{6,8},{7,9},{8,10},{9,11},{10,... | collective-permute-start | bytes 1769480 | tf_op jit(solution)/shard_map/ppermute | solution.py:17
  46.8 18.2 %copy-start.9 = (bf16[384,768]{1,0:T(8,128)(2,1)}, bf16[384,768]{1,0:T(8,128)(2,1)S(1)}, u32[]{:S(2)}) copy-start(bf16[384,768]{1,0:T(8,128)(2,1)S(1)} %collective-permute-done.1) | copy-start | bytes 1769476
  46.9 62.8 %collective-permute-start.8 = (bf16[384,1024]{1,0:T(8,128)(2,1)S(1)}, bf16[384,1024]{1,0:T(8,128)(2,1)}, u32[]{:S(2)}, u32[]{:S(2)}) collective-permute-start(bf16[384,1024]{1,0:T(8,128)(2,1)S(1)} %fusion.36), channel_id=1, source_target_pairs={{0,2},{1,3},{2,4},{3,5},{4,6},{5,7},{6,8},{7,9},{8,10},{9,11},{10,... | collective-permute-start | bytes 2359304 | tf_op jit(solution)/shard_map/ppermute | solution.py:17
  52.2 12.9 %copy-start.7 = (bf16[384,768]{1,0:T(8,128)(2,1)}, bf16[384,768]{1,0:T(8,128)(2,1)S(1)}, u32[]{:S(2)}) copy-start(bf16[384,768]{1,0:T(8,128)(2,1)S(1)} %collective-permute-done.4) | copy-start | bytes 1769476
  52.2 76.8 %collective-permute-start.11 = (bf16[384,1024]{1,0:T(8,128)(2,1)S(1)}, bf16[384,1024]{1,0:T(8,128)(2,1)}, u32[]{:S(2)}, u32[]{:S(2)}) collective-permute-start(bf16[384,1024]{1,0:T(8,128)(2,1)S(1)} %fusion.36), channel_id=1, source_target_pairs={{0,62},{1,63},{2,0},{3,1},{4,2},{5,3},{6,4},{7,5},{8,6},{9,7},{10,... | collective-permute-start | bytes 2359304 | tf_op jit(solution)/shard_map/ppermute | solution.py:17
  65.0 0.8 copy-start.5
  65.9 71.1 %collective-permute-start.14 = (bf16[384,1024]{1,0:T(8,128)(2,1)S(1)}, bf16[384,1024]{1,0:T(8,128)(2,1)}, u32[]{:S(2)}, u32[]{:S(2)}) collective-permute-start(bf16[384,1024]{1,0:T(8,128)(2,1)S(1)} %fusion.36), channel_id=1, source_target_pairs={{0,64},{64,0},{128,192},{192,128},{256,320},{320,256},{384,448},{4... | collective-permute-start | bytes 2359304 | tf_op jit(solution)/shard_map/ppermute | solution.py:27
  68.1 60.8 %collective-permute-start.10 = (bf16[384,768]{1,0:T(8,128)(2,1)S(1)}, bf16[384,768]{1,0:T(8,128)(2,1)}, u32[]{:S(2)}, u32[]{:S(2)}) collective-permute-start(bf16[384,768]{1,0:T(8,128)(2,1)S(1)} %fusion.38), channel_id=1, source_target_pairs={{0,62},{1,63},{2,0},{3,1},{4,2},{5,3},{6,4},{7,5},{8,6},{9,7},{10,... | collective-permute-start | bytes 1769480 | tf_op jit(solution)/shard_map/ppermute | solution.py:17
  95.3 5.8 %copy-start.11 = (bf16[384,1024]{1,0:T(8,128)(2,1)}, bf16[384,1024]{1,0:T(8,128)(2,1)S(1)}, u32[]{:S(2)}) copy-start(bf16[384,1024]{1,0:T(8,128)(2,1)S(1)} %collective-permute-done.5) | copy-start | bytes 2359300
  95.3 41.6 %collective-permute-start.13 = (bf16[384,768]{1,0:T(8,128)(2,1)S(1)}, bf16[384,768]{1,0:T(8,128)(2,1)}, u32[]{:S(2)}, u32[]{:S(2)}) collective-permute-start(bf16[384,768]{1,0:T(8,128)(2,1)S(1)} %fusion.38), channel_id=1, source_target_pairs={{0,64},{64,0},{128,192},{192,128},{256,320},{320,256},{384,448},{4... | collective-permute-start | bytes 1769480 | tf_op jit(solution)/shard_map/ppermute | solution.py:27
  103.6 0.9 copy-start.12
  103.6 2.6 copy-start.10
  109.1 4.0 %copy-start.1 = (f32[384,768]{1,0:T(8,128)}, f32[384,768]{1,0:T(8,128)S(1)}, u32[]{:S(2)}) copy-start(f32[384,768]{1,0:T(8,128)S(1)} %get-tuple-element.107) | copy-start | bytes 3538948
  109.7 27.2 %collective-permute-start.12 = (bf16[384]{0:T(512)(128)(2,1)S(1)}, bf16[384]{0:T(512)(128)(2,1)S(1)}, u32[]{:S(2)}, u32[]{:S(2)}) collective-permute-start(bf16[384]{0:T(512)(128)(2,1)S(1)} %get-tuple-element.141), channel_id=1, source_target_pairs={{0,64},{64,0},{128,192},{192,128},{256,320},{320,256},{384,448},{4... | collective-permute-start | bytes 2312 | tf_op jit(solution)/shard_map/ppermute | solution.py:27
  113.1 1.8 copy-start.8
  119.0 1.8 copy-start.6
  123.8 5.2 %copy-start.2 = (f32[384,768]{1,0:T(8,128)}, f32[384,768]{1,0:T(8,128)S(1)}, u32[]{:S(2)}) copy-start(f32[384,768]{1,0:T(8,128)S(1)} %get-tuple-element.109) | copy-start | bytes 3538948
  137.1 1.0 copy-start.3
